TPU v7x, 32 devices: a whole 2x2x4 slice. The times are simulated.
32 devices in a mesh: snap: 8 (over z, x), feat: 4 (over y, core).
Axes of the slice: x: 2, y: 2, z: 4, core: 2. Of those that a mesh axis runs over, the one named last changes fastest.
Arguments:
- node_features: bfloat16 [16, 512, 256], P('snap', None, 'feat'), may hold values from -6 to 6
- tile_rows: int32 [16, 8], P('snap'), may hold values from 0 to 3
- tile_cols: int32 [16, 8], P('snap'), may hold values from 0 to 3, as said below
- tile_counts: int32 [16], P('snap'), may hold values from 4 to 8, as said below
- tile_values: bfloat16 [16, 8, 128, 128], P('snap'), may hold values from -0.5 to 0.5
- layer_one: bfloat16 [256, 256], replicated, may hold values from -0.375 to 0.375
- layer_two: bfloat16 [256, 256], replicated, may hold values from -0.375 to 0.375
- query_weight: bfloat16 [256, 256], replicated, may hold values from -1.25 to 1.25
- key_weight: bfloat16 [256, 256], replicated, may hold values from -1.25 to 1.25
- value_weight: bfloat16 [256, 256], replicated, may hold values from -0.375 to 0.375
- out_weight: bfloat16 [256, 256], replicated, may hold values from -0.375 to 0.375
Outputs:
- evolved: bfloat16 [16, 512, 256], P('snap', None, 'feat')
Inputs may be any that keep to these rules, and one draw needn't show every extreme that they name: `tile_cols`: block columns of the tile slots; a coordinate pair may be listed more than once, and such tiles add. `tile_counts`: some snapshot uses all 8 slots.
All inputs are finite; a program needn't handle non-finite values.
Results may differ from a plain program's by a relative error of at most 0.02.
The roundings to bfloat16 on the way count: a program that leaves them out, or rounds other values in their place, can miss the bound.
Values may be sent and summed in bfloat16 or wider, within the bound.
A program may use at most 64 MiB of HBM per device.

v0:
```python
import jax
import jax.numpy as jnp
from jax import lax
from jax.sharding import PartitionSpec as P

HEADS = 8
masked_score = -1e30


def spread_padded(features, tile_block, block_rows, block_cols, slot_count):
    vert_count, feat_width = features.shape
    tile_side = tile_block.shape[1]
    slot_total = tile_block.shape[0]
    block_count = vert_count // tile_side
    blocked = features.reshape(block_count, tile_side, feat_width)
    picked_blocks = blocked[block_cols]
    live_slots = jnp.arange(slot_total, dtype=jnp.int32) < slot_count
    products = jnp.einsum(
        "irc,icf->irf", tile_block, picked_blocks, preferred_element_type=jnp.float32
    )
    products = products * live_slots.astype(jnp.float32)[:, None, None]
    membership = (
        (block_rows[None, :] == jnp.arange(block_count, dtype=jnp.int32)[:, None])
        & live_slots[None, :]
    ).astype(jnp.float32)
    summed = jnp.dot(
        membership,
        products.reshape(slot_total, tile_side * feat_width),
        precision=lax.Precision.HIGHEST,
    )
    return summed.reshape(vert_count, feat_width).astype(jnp.bfloat16)


def attend_local(hidden, query_weight, key_weight, value_weight, out_weight):
    snaps, verts, model_width = hidden.shape
    head_dim = model_width // HEADS
    flat = hidden.reshape(snaps * verts, model_width)

    def project(weight):
        return (
            jnp.dot(flat, weight, preferred_element_type=jnp.float32)
            .astype(jnp.bfloat16)
            .reshape(snaps, verts, HEADS, head_dim)
        )

    query_heads = project(query_weight)
    key_heads = project(key_weight)
    value_heads = project(value_weight)
    scores = jnp.einsum(
        "tvhd,uvhd->vhtu", query_heads, key_heads, preferred_element_type=jnp.float32
    ) * head_dim ** (-0.5)
    causal = (
        jnp.arange(snaps, dtype=jnp.int32)[:, None] >= jnp.arange(snaps, dtype=jnp.int32)[None, :]
    )
    scores = jnp.where(causal, scores, masked_score)
    row_max = jnp.max(scores, axis=-1, keepdims=True)
    lifted = jnp.exp(scores - row_max)
    weights = (lifted / jnp.sum(lifted, axis=-1, keepdims=True)).astype(jnp.bfloat16)
    context = jnp.einsum(
        "vhtu,uvhd->tvhd", weights, value_heads, preferred_element_type=jnp.float32
    ).astype(jnp.bfloat16)
    context = context.reshape(snaps * verts, model_width)
    result = flat.astype(jnp.float32) + jnp.dot(
        context, out_weight, preferred_element_type=jnp.float32
    )
    return result.astype(jnp.bfloat16).reshape(snaps, verts, model_width)


def on_device(
    node_features,
    tile_rows,
    tile_cols,
    tile_counts,
    tile_values,
    layer_one,
    layer_two,
    query_weight,
    key_weight,
    value_weight,
    out_weight,
):
    snap_dev, vert_count, feat_width = node_features.shape
    feat_index = lax.axis_index("feat")

    def spread_all(features):
        spread_pieces = []
        for snapshot in range(snap_dev):
            spread_pieces.append(
                spread_padded(
                    features[snapshot],
                    tile_values[snapshot],
                    tile_rows[snapshot],
                    tile_cols[snapshot],
                    tile_counts[snapshot],
                )
            )
        return jnp.stack(spread_pieces, axis=0)

    def convolve(features, weight):
        spread_rows = spread_all(features).reshape(snap_dev * vert_count, feat_width)
        own_columns = lax.dynamic_slice_in_dim(weight, feat_index * feat_width, feat_width, 1)
        mixed_sum = jnp.dot(
            lax.all_gather(spread_rows, "feat", axis=1, tiled=True),
            own_columns,
            preferred_element_type=jnp.float32,
        )
        mixed_sum = mixed_sum.reshape(snap_dev, vert_count, feat_width)
        return (features.astype(jnp.float32) + jnp.maximum(mixed_sum, 0.0)).astype(jnp.bfloat16)

    hidden_one = convolve(node_features, layer_one)
    hidden_two = convolve(hidden_one, layer_two)
    vertex_rows = lax.all_to_all(
        lax.all_to_all(hidden_two, "snap", split_axis=1, concat_axis=0, tiled=True),
        "feat",
        split_axis=1,
        concat_axis=2,
        tiled=True,
    )
    attended = attend_local(vertex_rows, query_weight, key_weight, value_weight, out_weight)
    return lax.all_to_all(
        lax.all_to_all(attended, "feat", split_axis=2, concat_axis=1, tiled=True),
        "snap",
        split_axis=0,
        concat_axis=1,
        tiled=True,
    )


def solution(mesh):
    placed = (
        P("snap", None, "feat"),
        P("snap", None),
        P("snap", None),
        P("snap"),
        P("snap", None, None, None),
        P(),
        P(),
        P(),
        P(),
        P(),
        P(),
    )
    return jax.shard_map(
        on_device, mesh=mesh, in_specs=placed, out_specs=P("snap", None, "feat"), check_vma=False
    )
```

profile of v0, /device:TPU:0, one launch (start us, length us, event | category | flops | bytes accessed | tf_op | source)
XLA Modules:
  0.0 81.3 jit_solution(12368943352257759503)
XLA Ops:
  0.0 0.7 copy-done.9
  0.7 0.9 %fusion.47 = (bf16[1,512,64]{1,2,0:T(8,128)(2,1)S(1)}, bf16[1,512,64]{1,2,0:T(8,128)(2,1)S(1)}) fusion(bf16[2,512,64]{1,2,0:T(8,128)(2,1)} %param.11), kind=kLoop, calls=%fused_computation.79 | loop fusion | bytes 262144 | tf_op jit(solution)/shard_map/slice | solution.py:90
  1.7 0.6 copy-done.8
  2.4 0.6 fusion.48
  3.0 0.6 iota_compare_fusion.4
  3.6 0.6 gather_fusion
  4.2 0.3 fusion.8
  4.9 0.5 copy-done.10
  5.4 0.2 convolution_convert_fusion.3
  5.9 0.6 iota_compare_fusion.3
  6.5 0.6 gather_fusion.1
  7.1 0.3 fusion.7
  7.8 0.2 convolution_convert_fusion.2
  8.4 8.7 %all_gather.6 = bf16[1024,256]{0,1:T(8,128)(2,1)S(1)} all-gather(bf16[1024,64]{0,1:T(8,128)(2,1)S(1)} %copy.107), channel_id=1, replica_groups=mesh['snap'=8,'feat'=4] {'feat'}, dimensions={1}, use_global_device_ids=true | all-gather | bytes 655360 | tf_op jit(solution)/shard_map/all_gather | solution.py:103
  17.1 0.3 convolution_maximum_fusion.1
  17.4 0.6 copy-done.2
  18.1 0.6 gather_fusion.2
  18.6 0.3 fusion.6
  19.3 0.2 convolution_convert_fusion.1
  19.8 0.6 gather_fusion.3
  20.4 0.3 fusion.5
  21.0 0.2 convolution_convert_fusion
  21.7 7.4 %all_gather.7 = bf16[1024,256]{0,1:T(8,128)(2,1)S(1)} all-gather(bf16[1024,64]{0,1:T(8,128)(2,1)S(1)} %copy.113), channel_id=1, replica_groups=mesh['snap'=8,'feat'=4] {'feat'}, dimensions={1}, use_global_device_ids=true | all-gather | bytes 655360 | tf_op jit(solution)/shard_map/all_gather | solution.py:103
  29.1 0.3 convolution_maximum_fusion
  29.6 0.2 reshape.211
  29.9 13.1 %all_to_all.69 = bf16[8,2,4096]{2,1,0:T(2,128)(2,1)S(1)} all-to-all(bf16[8,2,4096]{2,1,0:T(2,128)(2,1)S(1)} %reshape.211), channel_id=1, replica_groups=mesh['snap'=8,'feat'=4] {'snap'}, dimensions={0} | all-to-all | bytes 262144 | tf_op jit(solution)/shard_map/all_to_all | solution.py:113
  43.4 0.9 %reshape.213 = bf16[4,2,8192]{2,1,0:T(2,128)(2,1)} reshape(bf16[64,16,64]{2,1,0:T(8,128)(2,1)S(1)} %bitcast.111) | data formatting | bytes 262144
  44.3 3.3 %all-to-all-start.1 = ((bf16[4,2,8192]{2,1,0:T(2,128)(2,1)}), bf16[4,2,8192]{2,1,0:T(2,128)(2,1)S(1)}, u32[]{:S(2)}, u32[]{:S(2)}) async-start(bf16[4,2,8192]{2,1,0:T(2,128)(2,1)} %reshape.213), calls=%async_computation.1 | async-start | bytes 262144 | tf_op jit(solution)/shard_map/all_to_all | solution.py:112
  47.7 4.6 %all-to-all-done.1 = bf16[4,2,8192]{2,1,0:T(2,128)(2,1)S(1)} async-done(((bf16[4,2,8192]{2,1,0:T(2,128)(2,1)}), bf16[4,2,8192]{2,1,0:T(2,128)(2,1)S(1)}, u32[]{:S(2)}, u32[]{:S(2)}) %all-to-all-start.1) | async-done | bytes 131104 | tf_op jit(solution)/shard_map/all_to_all | solution.py:112
  52.7 0.2 reshape.173
  52.9 0.7 copy-done.3
  53.8 0.2 reshape.175
  54.0 0.7 copy-done.4
  54.9 0.2 reshape.176
  55.1 0.7 copy-done.5
  55.9 0.2 reshape.174
  56.2 1.0 %fusion.49 = (f32[16,8,16]{2,1,0:T(8,128)S(1)}, f32[16,8,16,16]{2,3,1,0:T(8,128)S(1)}) fusion(bf16[16,16,8,32]{3,2,1,0:T(8,128)(2,1)S(1)} %reshape.176, bf16[16,16,8,32]{3,2,1,0:T(8,128)(2,1)S(1)} %reshape.175, pred[16,16]{0,1:T(8,128)(4,1)S(1)} %iota_compare_fusion), kind=kOutput, calls=%fused_computation.81 | convolution fusion | flops 2228239 | bytes 401664 | tf_op jit(solution)/shard_map/sub | solution.py:57
  57.2 0.5 fusion.4
  57.9 0.4 reshape.177
  58.3 0.5 copy-done.6
  59.0 0.9 %copy.126 = bf16[16,16,256]{1,0,2:T(8,128)(2,1)S(1)} copy(bf16[16,16,256]{2,1,0:T(8,128)(2,1)S(1)} %bitcast.115) | data formatting | bytes 262144 | tf_op jit(solution)/shard_map/reshape | solution.py:66
  60.0 1.1 %reshape.215 = bf16[4,2,8192]{2,1,0:T(2,128)(2,1)S(1)} reshape(bf16[256,16,16]{2,1,0:T(8,128)(2,1)S(1)} %bitcast.102) | data formatting | bytes 262144
  61.0 7.0 %all_to_all.70 = bf16[4,2,8192]{2,1,0:T(2,128)(2,1)S(1)} all-to-all(bf16[4,2,8192]{2,1,0:T(2,128)(2,1)S(1)} %reshape.215), channel_id=1, replica_groups=mesh['snap'=8,'feat'=4] {'feat'}, dimensions={0} | all-to-all | bytes 262144 | tf_op jit(solution)/shard_map/all_to_all | solution.py:121
  68.0 0.7 reshape.216
  68.7 1.2 %copy.134 = bf16[16,16,4,64]{3,2,1,0:T(4,128)(2,1)S(1)} copy(bf16[16,16,4,64]{1,0,3,2:T(8,128)(2,1)S(1)} %bitcast.101) | data formatting | bytes 262144 | tf_op jit(solution)/shard_map/all_to_all | solution.py:121
  69.9 0.2 reshape.217
  70.2 9.9 %all_to_all.71 = bf16[8,2,4096]{2,1,0:T(2,128)(2,1)S(1)} all-to-all(bf16[8,2,4096]{2,1,0:T(2,128)(2,1)S(1)} %reshape.217), channel_id=1, replica_groups=mesh['snap'=8,'feat'=4] {'snap'}, dimensions={0} | all-to-all | bytes 262144 | tf_op jit(solution)/shard_map/all_to_all | solution.py:120
  80.5 0.9 %all_to_all.64 = bf16[2,512,64]{1,2,0:T(8,128)(2,1)} reshape(bf16[2,8,64,64]{2,1,3,0:T(8,128)(2,1)S(1)} %copy.129) | data formatting | bytes 262144 | tf_op jit(solution)/shard_map/all_to_all | solution.py:120
  (59 shorter events, 5.2 us)
Async XLA Ops:
  0.0 17.1 %copy-start = (bf16[256,256]{1,0:T(8,128)(2,1)S(1)}, bf16[256,256]{1,0:T(8,128)(2,1)}, u32[]{:S(2)}) copy-start(bf16[256,256]{1,0:T(8,128)(2,1)} %param.16) | copy-start | bytes 393220
  0.0 0.7 copy-start.9
  0.7 3.5 %copy-start.1 = (bf16[2,8,128,128]{3,2,1,0:T(8,128)(2,1)S(1)}, bf16[2,8,128,128]{3,2,1,0:T(8,128)(2,1)}, u32[]{:S(2)}) copy-start(bf16[2,8,128,128]{3,2,1,0:T(8,128)(2,1)} %param.15) | copy-start | bytes 1572868
  1.7 0.7 copy-start.8
  4.7 0.7 copy-start.10
  17.1 0.9 %copy-start.2 = (bf16[2,512,64]{1,2,0:T(8,128)(2,1)S(1)}, bf16[2,512,64]{1,2,0:T(8,128)(2,1)}, u32[]{:S(2)}) copy-start(bf16[2,512,64]{1,2,0:T(8,128)(2,1)} %param.11) | copy-start | bytes 393220
  21.7 7.4 %copy-start.7 = (bf16[256,256]{1,0:T(8,128)(2,1)S(1)}, bf16[256,256]{1,0:T(8,128)(2,1)}, u32[]{:S(2)}) copy-start(bf16[256,256]{1,0:T(8,128)(2,1)} %param.17) | copy-start | bytes 393220
  44.3 7.9 %all-to-all-start.1 = ((bf16[4,2,8192]{2,1,0:T(2,128)(2,1)}), bf16[4,2,8192]{2,1,0:T(2,128)(2,1)S(1)}, u32[]{:S(2)}, u32[]{:S(2)}) async-start(bf16[4,2,8192]{2,1,0:T(2,128)(2,1)} %reshape.213), calls=%async_computation.1 | async-start | bytes 262144 | tf_op jit(solution)/shard_map/all_to_all | solution.py:112
  52.7 0.9 %copy-start.3 = (bf16[256,256]{1,0:T(8,128)(2,1)S(1)}, bf16[256,256]{1,0:T(8,128)(2,1)}, u32[]{:S(2)}) copy-start(bf16[256,256]{1,0:T(8,128)(2,1)} %param.18) | copy-start | bytes 393220
  53.8 0.9 %copy-start.4 = (bf16[256,256]{1,0:T(8,128)(2,1)S(1)}, bf16[256,256]{1,0:T(8,128)(2,1)}, u32[]{:S(2)}) copy-start(bf16[256,256]{1,0:T(8,128)(2,1)} %param.19) | copy-start | bytes 393220
  54.9 0.9 %copy-start.5 = (bf16[256,256]{1,0:T(8,128)(2,1)S(1)}, bf16[256,256]{1,0:T(8,128)(2,1)}, u32[]{:S(2)}) copy-start(bf16[256,256]{1,0:T(8,128)(2,1)} %param.20) | copy-start | bytes 393220
  57.9 0.9 %copy-start.6 = (bf16[256,256]{1,0:T(8,128)(2,1)S(1)}, bf16[256,256]{1,0:T(8,128)(2,1)}, u32[]{:S(2)}) copy-start(bf16[256,256]{1,0:T(8,128)(2,1)} %param.21) | copy-start | bytes 393220
where the time goes:
time: 81.8 us; the launch traced here: 81.3 us
  blocking collectives  46 us (56%)
  local copies, waits for them, and re-layouts  20.4 us (25%)
  matrix products  4.96 us (6%)
  waiting for transfers between devices  4.55 us (6%)
  starting transfers between devices  3.33 us (4%)
  other arithmetic  1.48 us (2%)
    all_gather x2, blocking collectives, convolve(): lax.all_gather(spread_rows, 'feat', axis=1, tiled=True)  16.1 us
    all_to_all x1, blocking collectives, on_device(): lax.all_to_all(hidden_two, 'snap', split_axis=1, concat_axis=0, tiled=True)  13.1 us
    all_to_all x1, blocking collectives, on_device(): lax.all_to_all(lax.all_to_all(attended, 'feat', split_axis=2, concat_axis...  9.86 us
    unnamed x30, local copies, waits for them, and re-layouts  8.75 us
    all_to_all x1, blocking collectives, on_device(): lax.all_to_all(attended, 'feat', split_axis=2, concat_axis=1, tiled=True)  6.99 us
    all_to_all x1, waiting for transfers between devices, on_device(): lax.all_to_all(lax.all_to_all(hidden_two, 'snap', split_axis=1, concat_ax...  4.55 us
    all_to_all x1, starting transfers between devices, on_device(): lax.all_to_all(lax.all_to_all(hidden_two, 'snap', split_axis=1, concat_ax...  3.33 us
    gather x4, local copies, waits for them, and re-layouts, spread_padded(): picked_blocks = blocked[block_cols]  2.29 us
  transfers between devices with their start and end apart: 1, of which 1 were waited for; matrix products, arithmetic and copies ran while one was open for 0% of the time, Pallas kernels for 0%

commit v1 on v0

--- a/solution.py
+++ b/solution.py
@@ -100,7 +100,7 @@
         spread_rows = spread_all(features).reshape(snap_dev * vert_count, feat_width)
         own_columns = lax.dynamic_slice_in_dim(weight, feat_index * feat_width, feat_width, 1)
         mixed_sum = jnp.dot(
-            lax.all_gather(spread_rows, "feat", axis=1, tiled=True),
+            jnp.concatenate(lax.all_gather(spread_rows, "feat"), axis=1),
             own_columns,
             preferred_element_type=jnp.float32,
         )

time: 81.8 us -> 82.9 us (1.013)
  local copies, waits for them, and re-layouts: 20.4 us -> 21.6 us
where the time goes in v1:
time: 82.9 us; the launch traced here: 82.3 us
  blocking collectives  45.9 us (55%)
  local copies, waits for them, and re-layouts  21.6 us (26%)
  matrix products  4.97 us (6%)
  waiting for transfers between devices  4.37 us (5%)
  starting transfers between devices  3.51 us (4%)
  other arithmetic  1.42 us (2%)
    all_gather x2, blocking collectives, convolve(): lax.all_gather(spread_rows, 'feat')  16 us
    all_to_all x1, blocking collectives, on_device(): lax.all_to_all(hidden_two, 'snap', split_axis=1, concat_axis=0, tiled=True)  13.1 us
    all_to_all x1, blocking collectives, on_device(): lax.all_to_all(lax.all_to_all(attended, 'feat', split_axis=2, concat_axis...  9.85 us
    unnamed x30, local copies, waits for them, and re-layouts  9.2 us
    all_to_all x1, blocking collectives, on_device(): lax.all_to_all(attended, 'feat', split_axis=2, concat_axis=1, tiled=True)  6.99 us
    all_to_all x1, waiting for transfers between devices, on_device(): lax.all_to_all(lax.all_to_all(hidden_two, 'snap', split_axis=1, concat_ax...  4.37 us
    all_to_all x1, starting transfers between devices, on_device(): lax.all_to_all(lax.all_to_all(hidden_two, 'snap', split_axis=1, concat_ax...  3.51 us
    gather x4, local copies, waits for them, and re-layouts, spread_padded(): picked_blocks = blocked[block_cols]  2.29 us
  transfers between devices with their start and end apart: 1, of which 1 were waited for; matrix products, arithmetic and copies ran while one was open for 0% of the time, Pallas kernels for 0%

profile of v1, /device:TPU:0, one launch (start us, length us, event | category | flops | bytes accessed | tf_op | source)
XLA Modules:
  0.0 82.3 jit_solution(11732548535319540781)
XLA Ops:
  0.0 0.7 copy-done.8
  0.7 0.9 %fusion.53 = (bf16[1,512,64]{1,2,0:T(8,128)(2,1)S(1)}, bf16[1,512,64]{1,2,0:T(8,128)(2,1)S(1)}) fusion(bf16[2,512,64]{1,2,0:T(8,128)(2,1)} %param.11), kind=kLoop, calls=%fused_computation.83 | loop fusion | bytes 262144 | tf_op jit(solution)/shard_map/slice | solution.py:90
  1.7 0.6 copy-done.7
  2.4 0.6 fusion.54
  3.0 0.6 iota_compare_fusion.4
  3.6 0.6 gather_fusion
  4.2 0.3 fusion.10
  4.9 0.5 copy-done.9
  5.4 0.2 convolution_convert_fusion.3
  5.9 0.6 iota_compare_fusion.3
  6.5 0.6 gather_fusion.1
  7.1 0.3 fusion.9
  7.8 0.2 convolution_convert_fusion.2
  8.4 8.7 %all_gather.6 = bf16[4,1024,64]{1,2,0:T(8,128)(2,1)S(1)} all-gather(bf16[1,1024,64]{1,2,0:T(8,128)(2,1)S(1)} %copy.93), channel_id=1, replica_groups=mesh['snap'=8,'feat'=4] {'feat'}, dimensions={0}, use_global_device_ids=true | all-gather | bytes 655360 | tf_op jit(solution)/shard_map/all_gather | solution.py:103
  17.1 0.4 dot_general.56
  17.5 0.5 copy-done.5
  18.0 0.3 fusion.11
  18.4 0.6 gather_fusion.2
  18.9 0.3 fusion.7
  19.6 0.2 convolution_convert_fusion.1
  20.1 0.6 gather_fusion.3
  20.7 0.3 fusion.6
  21.3 0.2 convolution_convert_fusion
  22.0 7.3 %all_gather.7 = bf16[4,1024,64]{1,2,0:T(8,128)(2,1)S(1)} all-gather(bf16[1,1024,64]{1,2,0:T(8,128)(2,1)S(1)} %copy.100), channel_id=1, replica_groups=mesh['snap'=8,'feat'=4] {'feat'}, dimensions={0}, use_global_device_ids=true | all-gather | bytes 655360 | tf_op jit(solution)/shard_map/all_gather | solution.py:103
  29.2 0.4 dot_general.62
  29.6 0.5 copy-done.10
  30.1 0.3 fusion.12
  30.6 0.2 reshape.215
  30.9 13.1 %all_to_all.69 = bf16[8,2,4096]{2,1,0:T(2,128)(2,1)S(1)} all-to-all(bf16[8,2,4096]{2,1,0:T(2,128)(2,1)S(1)} %reshape.215), channel_id=1, replica_groups=mesh['snap'=8,'feat'=4] {'snap'}, dimensions={0} | all-to-all | bytes 262144 | tf_op jit(solution)/shard_map/all_to_all | solution.py:113
  44.4 0.9 %reshape.217 = bf16[4,2,8192]{2,1,0:T(2,128)(2,1)} reshape(bf16[64,16,64]{2,1,0:T(8,128)(2,1)S(1)} %bitcast.113) | data formatting | bytes 262144
  45.3 3.5 %all-to-all-start.1 = ((bf16[4,2,8192]{2,1,0:T(2,128)(2,1)}), bf16[4,2,8192]{2,1,0:T(2,128)(2,1)S(1)}, u32[]{:S(2)}, u32[]{:S(2)}) async-start(bf16[4,2,8192]{2,1,0:T(2,128)(2,1)} %reshape.217), calls=%async_computation.1 | async-start | bytes 262144 | tf_op jit(solution)/shard_map/all_to_all | solution.py:112
  48.9 4.4 %all-to-all-done.1 = bf16[4,2,8192]{2,1,0:T(2,128)(2,1)S(1)} async-done(((bf16[4,2,8192]{2,1,0:T(2,128)(2,1)}), bf16[4,2,8192]{2,1,0:T(2,128)(2,1)S(1)}, u32[]{:S(2)}, u32[]{:S(2)}) %all-to-all-start.1) | async-done | bytes 131104 | tf_op jit(solution)/shard_map/all_to_all | solution.py:112
  53.9 0.7 copy-done.2
  54.8 0.2 reshape.177
  55.0 0.7 copy-done.3
  56.1 0.7 copy-done.4
  57.2 1.0 %fusion.55 = (f32[16,8,16]{2,1,0:T(8,128)S(1)}, f32[16,8,16,16]{2,3,1,0:T(8,128)S(1)}) fusion(bf16[16,16,8,32]{3,2,1,0:T(8,128)(2,1)S(1)} %reshape.178, bf16[16,16,8,32]{3,2,1,0:T(8,128)(2,1)S(1)} %reshape.177, pred[16,16]{0,1:T(8,128)(4,1)S(1)} %iota_compare_fusion), kind=kOutput, calls=%fused_computation.85 | convolution fusion | flops 2228239 | bytes 401664 | tf_op jit(solution)/shard_map/sub | solution.py:57
  58.3 0.5 fusion.4
  58.9 0.4 reshape.179
  59.3 0.5 copy-done.6
  60.0 0.9 %copy.114 = bf16[16,16,256]{1,0,2:T(8,128)(2,1)S(1)} copy(bf16[16,16,256]{2,1,0:T(8,128)(2,1)S(1)} %bitcast.117) | data formatting | bytes 262144 | tf_op jit(solution)/shard_map/reshape | solution.py:66
  61.0 1.1 %reshape.219 = bf16[4,2,8192]{2,1,0:T(2,128)(2,1)S(1)} reshape(bf16[256,16,16]{2,1,0:T(8,128)(2,1)S(1)} %bitcast.104) | data formatting | bytes 262144
  62.0 7.0 %all_to_all.70 = bf16[4,2,8192]{2,1,0:T(2,128)(2,1)S(1)} all-to-all(bf16[4,2,8192]{2,1,0:T(2,128)(2,1)S(1)} %reshape.219), channel_id=1, replica_groups=mesh['snap'=8,'feat'=4] {'feat'}, dimensions={0} | all-to-all | bytes 262144 | tf_op jit(solution)/shard_map/all_to_all | solution.py:121
  69.0 0.7 reshape.220
  69.7 1.2 %copy.122 = bf16[16,16,4,64]{3,2,1,0:T(4,128)(2,1)S(1)} copy(bf16[16,16,4,64]{1,0,3,2:T(8,128)(2,1)S(1)} %bitcast.103) | data formatting | bytes 262144 | tf_op jit(solution)/shard_map/all_to_all | solution.py:121
  71.0 0.2 reshape.221
  71.2 9.9 %all_to_all.71 = bf16[8,2,4096]{2,1,0:T(2,128)(2,1)S(1)} all-to-all(bf16[8,2,4096]{2,1,0:T(2,128)(2,1)S(1)} %reshape.221), channel_id=1, replica_groups=mesh['snap'=8,'feat'=4] {'snap'}, dimensions={0} | all-to-all | bytes 262144 | tf_op jit(solution)/shard_map/all_to_all | solution.py:120
  81.5 0.9 %all_to_all.64 = bf16[2,512,64]{1,2,0:T(8,128)(2,1)} reshape(bf16[2,8,64,64]{2,1,3,0:T(8,128)(2,1)S(1)} %copy.117) | data formatting | bytes 262144 | tf_op jit(solution)/shard_map/all_to_all | solution.py:120
  (59 shorter events, 5.8 us)
Async XLA Ops:
  0.0 17.4 %copy-start = (bf16[256,256]{1,0:T(8,128)(2,1)S(1)}, bf16[256,256]{1,0:T(8,128)(2,1)}, u32[]{:S(2)}) copy-start(bf16[256,256]{1,0:T(8,128)(2,1)} %param.16) | copy-start | bytes 393220
  0.0 0.7 copy-start.8
  0.7 3.5 %copy-start.1 = (bf16[2,8,128,128]{3,2,1,0:T(8,128)(2,1)S(1)}, bf16[2,8,128,128]{3,2,1,0:T(8,128)(2,1)}, u32[]{:S(2)}) copy-start(bf16[2,8,128,128]{3,2,1,0:T(8,128)(2,1)} %param.15) | copy-start | bytes 1572868
  1.7 0.7 copy-start.7
  4.7 0.7 copy-start.9
  17.1 0.9 %copy-start.5 = (bf16[2,512,64]{1,2,0:T(8,128)(2,1)S(1)}, bf16[2,512,64]{1,2,0:T(8,128)(2,1)}, u32[]{:S(2)}) copy-start(bf16[2,512,64]{1,2,0:T(8,128)(2,1)} %param.11) | copy-start | bytes 393220
  29.2 0.9 %copy-start.10 = (bf16[256,256]{1,0:T(8,128)(2,1)S(1)}, bf16[256,256]{1,0:T(8,128)(2,1)}, u32[]{:S(2)}) copy-start(bf16[256,256]{1,0:T(8,128)(2,1)} %param.17) | copy-start | bytes 393220
  45.3 7.9 %all-to-all-start.1 = ((bf16[4,2,8192]{2,1,0:T(2,128)(2,1)}), bf16[4,2,8192]{2,1,0:T(2,128)(2,1)S(1)}, u32[]{:S(2)}, u32[]{:S(2)}) async-start(bf16[4,2,8192]{2,1,0:T(2,128)(2,1)} %reshape.217), calls=%async_computation.1 | async-start | bytes 262144 | tf_op jit(solution)/shard_map/all_to_all | solution.py:112
  53.7 0.9 %copy-start.2 = (bf16[256,256]{1,0:T(8,128)(2,1)S(1)}, bf16[256,256]{1,0:T(8,128)(2,1)}, u32[]{:S(2)}) copy-start(bf16[256,256]{1,0:T(8,128)(2,1)} %param.18) | copy-start | bytes 393220
  54.8 0.9 %copy-start.3 = (bf16[256,256]{1,0:T(8,128)(2,1)S(1)}, bf16[256,256]{1,0:T(8,128)(2,1)}, u32[]{:S(2)}) copy-start(bf16[256,256]{1,0:T(8,128)(2,1)} %param.19) | copy-start | bytes 393220
  55.9 0.9 %copy-start.4 = (bf16[256,256]{1,0:T(8,128)(2,1)S(1)}, bf16[256,256]{1,0:T(8,128)(2,1)}, u32[]{:S(2)}) copy-start(bf16[256,256]{1,0:T(8,128)(2,1)} %param.20) | copy-start | bytes 393220
  58.9 0.9 %copy-start.6 = (bf16[256,256]{1,0:T(8,128)(2,1)S(1)}, bf16[256,256]{1,0:T(8,128)(2,1)}, u32[]{:S(2)}) copy-start(bf16[256,256]{1,0:T(8,128)(2,1)} %param.21) | copy-start | bytes 393220
